TPU v7x, 256 devices: a whole 4x4x8 slice. The times are simulated.
256 devices in a mesh: row: 32 (over y, x, z_hi), col: 8 (over z_lo, core).
Axes of the slice: x: 4, y: 4, z: 8 (z_hi: 2, z_lo: 4; z = z_hi * 4 + z_lo), core: 2. Of those that a mesh axis runs over, the one named last changes fastest.
Arguments:
- hamiltonian_blocks: bfloat16 [32, 8, 64, 128, 128], P('row', 'col'), may hold values from -0.046875 to 0.046875
- block_rows: int32 [32, 8, 64], P('row', 'col'), may hold values from 0 to 7, as said below
- block_cols: int32 [32, 8, 64], P('row', 'col'), may hold values from 0 to 31
- block_counts: int32 [32, 8], P('row', 'col'), may hold values from 16 to 64, as said below
- initial: float32 [32768, 128], P(('row', 'col')), may hold values from -6 to 6
- center: float32 [1], replicated, may hold values from -0.3 to 0.3
- halfwidth: float32 [1], replicated, may hold values from 1 to 1.5
Outputs:
- filtered: float32 [32768, 128], P(('row', 'col'))
Inputs may be any that keep to these rules, and one draw needn't show every extreme that they name: `block_rows`: padded slots hold arbitrary values. `block_counts`: some tile is full in every draw.
All inputs are finite; a program needn't handle non-finite values.
Results may differ from a plain program's by a relative error of at most 0.0068.
Values may be sent and summed in bfloat16 or wider, within the bound.
A program may use at most 128 MiB of HBM per device.

v0:
```python
import jax
import jax.numpy as jnp
from jax import lax
from jax.sharding import PartitionSpec as P

SLAB = 1
DEGREE = 3


def body(hamiltonian_blocks, block_rows, block_cols, block_counts, initial, center, halfwidth):
    stacked = hamiltonian_blocks[0, 0]
    slot_rows = block_rows[0, 0]
    slot_cols = block_cols[0, 0]
    live_count = block_counts[0, 0]
    grid_rows = lax.axis_size("row")
    grid_cols = lax.axis_size("col")
    orbitals = stacked.shape[1]
    vectors = initial.shape[1]
    slots = stacked.shape[0]
    row_segments = grid_cols * SLAB
    col_segments = grid_rows * SLAB
    highest = lax.Precision.HIGHEST
    is_live = jnp.arange(slots, dtype=jnp.int32) < live_count
    row_onehot = (
        (slot_rows[None, :] == jnp.arange(row_segments, dtype=jnp.int32)[:, None])
        & is_live[None, :]
    ).astype(jnp.float32)
    col_onehot = (
        (slot_cols[None, :] == jnp.arange(col_segments, dtype=jnp.int32)[:, None])
        & is_live[None, :]
    ).astype(jnp.float32)
    previous = initial
    current = initial
    for degree_step in range(DEGREE):
        panel = current.astype(jnp.bfloat16)
        apply_column_panel = lax.all_gather(panel, "row", axis=0, tiled=True).reshape(
            -1, orbitals, vectors
        )
        apply_row_panel = lax.all_gather(panel, "col", axis=0, tiled=True).reshape(
            -1, orbitals, vectors
        )
        upper_products = jnp.einsum(
            "sab,sbv->sav",
            stacked,
            apply_column_panel[slot_cols],
            preferred_element_type=jnp.float32,
        )
        upper_partial = jnp.einsum("ts,sav->tav", row_onehot, upper_products, precision=highest)
        upper_sum = lax.psum_scatter(
            upper_partial.reshape(-1, vectors), "col", scatter_dimension=0, tiled=True
        )
        products = jnp.einsum(
            "sba,sbv->sav", stacked, apply_row_panel[slot_rows], preferred_element_type=jnp.float32
        )
        lower_partial = jnp.einsum("ts,sav->tav", col_onehot, products, precision=highest)
        lower_sum = lax.psum_scatter(
            lower_partial.reshape(-1, vectors), "row", scatter_dimension=0, tiled=True
        )
        applied = upper_sum + lower_sum
        shifted = (applied - center[0] * current) / halfwidth[0]
        if degree_step == 0:
            following = shifted
        else:
            following = 2.0 * shifted - previous
        previous = current
        current = following
    return current


def solution(mesh):
    in_specs = (
        P("row", "col", None, None, None),
        P("row", "col", None),
        P("row", "col", None),
        P("row", "col"),
        P(("row", "col"), None),
        P(),
        P(),
    )
    out_specs = P(("row", "col"), None)
    return jax.shard_map(body, mesh=mesh, in_specs=in_specs, out_specs=out_specs, check_vma=False)
```

profile of v0, /device:TPU:32, one launch (start us, length us, event | category | flops | bytes accessed | tf_op | source)
XLA Modules:
  0.0 1112.5 jit_solution(9385953845992300890)
XLA Ops:
  9.6 83.8 %all-gather.4.cloned.1.call-done = bf16[4096,128]{1,0:T(8,128)(2,1)} async-done(((bf16[128,128]{1,0:T(8,128)(2,1)}), bf16[4096,128]{1,0:T(8,128)(2,1)}) %all-gather.4.cloned.1.call-update) | async-done | bytes 1048592 | tf_op jit(solution)/shard_map/all_gather | solution.py:36
  96.8 5.2 fusion.22
  102.0 5.4 copy.14
  112.1 13.5 %all_gather.19 = bf16[1024,128]{1,0:T(8,128)(2,1)S(1)} all-gather(bf16[128,128]{1,0:T(8,128)(2,1)S(1)} %copy-done.2), channel_id=1, replica_groups=mesh['row'=32,'col'=8] {'col'}, dimensions={0}, use_global_device_ids=true | all-gather | bytes 294912 | tf_op jit(solution)/shard_map/all_gather | solution.py:39
  127.8 4.4 fusion.20
  132.2 5.4 copy.15
  137.6 4.0 fusion.8
  145.6 234.6 %reduce-scatter.9.cloned.1.call-done = f32[128,128]{1,0:T(8,128)} async-done(((f32[4096,128]{1,0:T(8,128)}), f32[128,128]{1,0:T(8,128)}) %reduce-scatter.9.cloned.1.call-update) | async-done | bytes 65552 | tf_op jit(solution)/shard_map/reduce_scatter | solution.py:56
  382.0 73.9 %all-gather.6.cloned.1.call-done = bf16[4096,128]{1,0:T(8,128)(2,1)} async-done(((bf16[128,128]{1,0:T(8,128)(2,1)}), bf16[4096,128]{1,0:T(8,128)(2,1)}) %all-gather.6.cloned.1.call-update) | async-done | bytes 1048592 | tf_op jit(solution)/shard_map/all_gather | solution.py:36
  459.3 5.2 fusion.18
  464.5 5.4 copy.16
  474.6 13.5 %all_gather.21 = bf16[1024,128]{1,0:T(8,128)(2,1)S(1)} all-gather(bf16[128,128]{1,0:T(8,128)(2,1)S(1)} %copy-done.3), channel_id=1, replica_groups=mesh['row'=32,'col'=8] {'col'}, dimensions={0}, use_global_device_ids=true | all-gather | bytes 294912 | tf_op jit(solution)/shard_map/all_gather | solution.py:39
  490.2 4.4 fusion.16
  494.6 5.4 copy.17
  500.1 4.0 fusion.4
  506.8 235.0 %reduce-scatter.13.cloned.1.call-done = f32[128,128]{1,0:T(8,128)} async-done(((f32[4096,128]{1,0:T(8,128)}), f32[128,128]{1,0:T(8,128)}) %reduce-scatter.13.cloned.1.call-update) | async-done | bytes 65552 | tf_op jit(solution)/shard_map/reduce_scatter | solution.py:56
  743.5 74.6 %all-gather.8.cloned.1.call-done = bf16[4096,128]{1,0:T(8,128)(2,1)} async-done(((bf16[128,128]{1,0:T(8,128)(2,1)}), bf16[4096,128]{1,0:T(8,128)(2,1)}) %all-gather.8.cloned.1.call-update) | async-done | bytes 1048592 | tf_op jit(solution)/shard_map/all_gather | solution.py:36
  821.5 5.2 fusion.14
  826.7 5.4 copy.18
  836.8 13.5 %all_gather.23 = bf16[1024,128]{1,0:T(8,128)(2,1)S(1)} all-gather(bf16[128,128]{1,0:T(8,128)(2,1)S(1)} %copy-done.4), channel_id=1, replica_groups=mesh['row'=32,'col'=8] {'col'}, dimensions={0}, use_global_device_ids=true | all-gather | bytes 294912 | tf_op jit(solution)/shard_map/all_gather | solution.py:39
  852.4 4.4 fusion.12
  856.8 5.4 copy.19
  862.3 4.0 fusion
  868.9 235.5 %reduce-scatter.17.cloned.1.call-done = f32[128,128]{1,0:T(8,128)} async-done(((f32[4096,128]{1,0:T(8,128)}), f32[128,128]{1,0:T(8,128)}) %reduce-scatter.17.cloned.1.call-update) | async-done | bytes 65552 | tf_op jit(solution)/shard_map/reduce_scatter | solution.py:56
  (59 shorter events, 46.0 us)
Async XLA Ops:
  6.5 90.3 %copy-start = (bf16[1,1,64,128,128]{4,3,2,1,0:T(8,128)(2,1)S(1)}, bf16[1,1,64,128,128]{4,3,2,1,0:T(8,128)(2,1)}, u32[]{:S(2)}) copy-start(bf16[1,1,64,128,128]{4,3,2,1,0:T(8,128)(2,1)} %param.7) | copy-start | bytes 6291460
  6.5 86.9 %all-gather.4.cloned.1.call-start = ((), (), s32[]{:S(2)}) async-start(), calls=%async_computation.6 | async-start | bytes 1081344 | tf_op jit(solution)/shard_map/all_gather | solution.py:36
  8.2 137.4 %reduce-scatter.7.cloned.1.call-start = ((), (), s32[]{:S(2)}) async-start(), calls=%async_computation.7 | async-start | bytes 589824 | tf_op jit(solution)/shard_map/reduce_scatter | solution.py:49
  102.0 5.4 copy-start.5
  107.4 4.7 copy-start.2
  112.0 268.2 %reduce-scatter.9.cloned.1.call-start = ((), (), s32[]{:S(2)}) async-start(), calls=%async_computation.8 | async-start | bytes 2162688 | tf_op jit(solution)/shard_map/reduce_scatter | solution.py:56
  132.2 5.4 copy-start.6
  144.2 236.0 %copy-start.1 = (f32[128,128]{1,0:T(8,128)S(1)}, f32[128,128]{1,0:T(8,128)}, u32[]{:S(2)}) copy-start(f32[128,128]{1,0:T(8,128)} %param.11) | copy-start | bytes 196612
  144.2 311.7 %all-gather.6.cloned.1.call-start = ((), (), s32[]{:S(2)}) async-start(), calls=%async_computation.9 | async-start | bytes 1081344 | tf_op jit(solution)/shard_map/all_gather | solution.py:36
  381.8 125.0 %reduce-scatter.11.cloned.1.call-start = ((), (), s32[]{:S(2)}) async-start(), calls=%async_computation.10 | async-start | bytes 589824 | tf_op jit(solution)/shard_map/reduce_scatter | solution.py:49
  469.9 4.7 copy-start.3
  474.5 267.2 %reduce-scatter.13.cloned.1.call-start = ((), (), s32[]{:S(2)}) async-start(), calls=%async_computation.11 | async-start | bytes 2162688 | tf_op jit(solution)/shard_map/reduce_scatter | solution.py:56
  506.7 311.4 %all-gather.8.cloned.1.call-start = ((), (), s32[]{:S(2)}) async-start(), calls=%async_computation.12 | async-start | bytes 1081344 | tf_op jit(solution)/shard_map/all_gather | solution.py:36
  743.2 125.7 %reduce-scatter.15.cloned.1.call-start = ((), (), s32[]{:S(2)}) async-start(), calls=%async_computation.13 | async-start | bytes 589824 | tf_op jit(solution)/shard_map/reduce_scatter | solution.py:49
  832.1 4.7 copy-start.4
  836.7 267.8 %reduce-scatter.17.cloned.1.call-start = ((), (), s32[]{:S(2)}) async-start(), calls=%async_computation.14 | async-start | bytes 2162688 | tf_op jit(solution)/shard_map/reduce_scatter | solution.py:56
Sparse Core Ops, SparseCore 0:
  10.7 82.6 all-gather.3
  112.1 28.7 reduce-scatter.6
  144.4 235.8 reduce-scatter.8
  383.5 72.3 all-gather.5
  474.6 28.6 reduce-scatter.10
  506.8 234.8 reduce-scatter.12
  745.1 72.9 all-gather.7
  836.8 28.6 reduce-scatter.14
  869.0 235.3 reduce-scatter.16
where the time goes:
time: 1110 us
  waiting for transfers between devices  938 us (85%)
  local copies, waits for them, and re-layouts  59.8 us (5%)
  matrix products  51.8 us (5%)
  blocking collectives  40.5 us (4%)
  between operations  15.3 us (1%)
    reduce_scatter x3, waiting for transfers between devices, body(): lax.psum_scatter(lower_partial.reshape(-1, vectors), 'row', scatter_dimen...  705 us
    all_gather x3, waiting for transfers between devices, body(): lax.all_gather(panel, 'row', axis=0, tiled=True)  232 us
    all_gather x3, blocking collectives, body(): lax.all_gather(panel, 'col', axis=0, tiled=True)  40.5 us
  transfers between devices with their start and end apart: 9, of which 6 were waited for; matrix products, arithmetic and copies ran while one was open for 5% of the time, Pallas kernels for 0%

commit v1 on v0

--- a/solution.py
+++ b/solution.py
@@ -5,6 +5,13 @@
 
 SLAB = 1
 DEGREE = 3
+
+
+def modes_assign(local_values, dim_i):
+    return jnp.concatenate(
+        lax.all_to_all(jnp.stack([local_values for _ in range(lax.axis_size("row"))]), "row", 0, 0),
+        axis=dim_i,
+    )
 
 
 def body(hamiltonian_blocks, block_rows, block_cols, block_counts, initial, center, halfwidth):
@@ -33,9 +40,7 @@
     current = initial
     for degree_step in range(DEGREE):
         panel = current.astype(jnp.bfloat16)
-        apply_column_panel = lax.all_gather(panel, "row", axis=0, tiled=True).reshape(
-            -1, orbitals, vectors
-        )
+        apply_column_panel = modes_assign(panel, dim_i=0).reshape(-1, orbitals, vectors)
         apply_row_panel = lax.all_gather(panel, "col", axis=0, tiled=True).reshape(
             -1, orbitals, vectors
         )

time: 1110 us -> 977 us (0.88)
  waiting for transfers between devices: 938 us -> 743 us
  blocking collectives: 40.5 us -> 90.6 us
  starting transfers between devices: 0.74 us -> 13.3 us
    all_gather x3 -> x0, waiting for transfers between devices: 232 us -> none  [body(): lax.all_gather(panel, 'row', axis=0, tiled=True)]
    all_to_all x0 -> x2, blocking collectives: none -> 52.4 us  [modes_assign(): lax.all_to_all(jnp.stack([local_values for _ in range(lax.axis_size('row'...]
    all_to_all x0 -> x1, waiting for transfers between devices: none -> 32.2 us  [modes_assign(): lax.all_to_all(jnp.stack([local_values for _ in range(lax.axis_size('row'...]
    all_to_all x0 -> x1, starting transfers between devices: none -> 13 us  [modes_assign(): lax.all_to_all(jnp.stack([local_values for _ in range(lax.axis_size('row'...]
  transfers between devices with their start and end apart: 9 -> 7, of which waited for: 6 -> 4; matrix products, arithmetic and copies ran while one was open for 5% -> 6% of each run, Pallas kernels for 0% -> 0%
where the time goes in v1:
time: 977 us; the launch traced here: 976 us
  waiting for transfers between devices  743 us (76%)
  blocking collectives  90.6 us (9%)
  local copies, waits for them, and re-layouts  57.4 us (6%)
  matrix products  51.7 us (5%)
  between operations  15.6 us (2%)
  starting transfers between devices  13.3 us (1%)
    reduce_scatter x3, waiting for transfers between devices, body(): lax.psum_scatter(lower_partial.reshape(-1, vectors), 'row', scatter_dimen...  711 us
    all_to_all x2, blocking collectives, modes_assign(): lax.all_to_all(jnp.stack([local_values for _ in range(lax.axis_size('row'...  52.4 us
    all_gather x3, blocking collectives, body(): lax.all_gather(panel, 'col', axis=0, tiled=True)  38.2 us
    all_to_all x1, waiting for transfers between devices, modes_assign(): lax.all_to_all(jnp.stack([local_values for _ in range(lax.axis_size('row'...  32.2 us
  transfers between devices with their start and end apart: 7, of which 4 were waited for; matrix products, arithmetic and copies ran while one was open for 6% of the time, Pallas kernels for 0%

profile of v1, /device:TPU:32, one launch (start us, length us, event | category | flops | bytes accessed | tf_op | source)
XLA Modules:
  0.0 975.8 jit_solution(2471129629645405920)
XLA Ops:
  8.8 13.0 %all-to-all-start = ((bf16[32,128,128]{2,1,0:T(8,128)(2,1)}), bf16[32,128,128]{2,1,0:T(8,128)(2,1)S(1)}, u32[]{:S(2)}, u32[]{:S(2)}) async-start(bf16[32,128,128]{2,1,0:T(8,128)(2,1)} %stack.6), calls=%async_computation | async-start | bytes 2097152 | tf_op jit(solution)/shard_map/all_to_all | solution.py:12
  22.5 32.2 %all-to-all-done = bf16[32,128,128]{2,1,0:T(8,128)(2,1)S(1)} async-done(((bf16[32,128,128]{2,1,0:T(8,128)(2,1)}), bf16[32,128,128]{2,1,0:T(8,128)(2,1)S(1)}, u32[]{:S(2)}, u32[]{:S(2)}) %all-to-all-start) | async-done | bytes 1048608 | tf_op jit(solution)/shard_map/all_to_all | solution.py:12
  56.9 5.1 fusion.22
  62.1 5.4 copy.14
  72.2 13.0 %all_gather.9 = bf16[1024,128]{1,0:T(8,128)(2,1)S(1)} all-gather(bf16[128,128]{1,0:T(8,128)(2,1)S(1)} %convert_element_type.11), channel_id=1, replica_groups=mesh['row'=32,'col'=8] {'col'}, dimensions={0}, use_global_device_ids=true | all-gather | bytes 294912 | tf_op jit(solution)/shard_map/all_gather | solution.py:44
  87.3 4.4 fusion.20
  91.7 5.4 copy.15
  97.1 4.0 fusion.8
  105.1 236.5 %reduce-scatter.9.cloned.1.call-done = f32[128,128]{1,0:T(8,128)} async-done(((f32[4096,128]{1,0:T(8,128)}), f32[128,128]{1,0:T(8,128)}) %reduce-scatter.9.cloned.1.call-update) | async-done | bytes 65552 | tf_op jit(solution)/shard_map/reduce_scatter | solution.py:61
  342.7 26.2 %all_to_all.15 = bf16[32,128,128]{2,1,0:T(8,128)(2,1)S(1)} all-to-all(bf16[32,128,128]{2,1,0:T(8,128)(2,1)S(1)} %stack.7), channel_id=1, replica_groups=mesh['row'=32,'col'=8] {'row'}, dimensions={0} | all-to-all | bytes 2097152 | tf_op jit(solution)/shard_map/all_to_all | solution.py:12
  371.1 5.1 fusion.18
  376.2 5.4 copy.16
  386.2 12.5 %all_gather.10 = bf16[1024,128]{1,0:T(8,128)(2,1)S(1)} all-gather(bf16[128,128]{1,0:T(8,128)(2,1)S(1)} %get-tuple-element.7), channel_id=1, replica_groups=mesh['row'=32,'col'=8] {'col'}, dimensions={0}, use_global_device_ids=true | all-gather | bytes 294912 | tf_op jit(solution)/shard_map/all_gather | solution.py:44
  400.9 4.4 fusion.16
  405.3 5.4 copy.17
  417.4 239.8 %reduce-scatter.13.cloned.1.call-done = f32[128,128]{1,0:T(8,128)} async-done(((f32[4096,128]{1,0:T(8,128)}), f32[128,128]{1,0:T(8,128)}) %reduce-scatter.13.cloned.1.call-update) | async-done | bytes 65552 | tf_op jit(solution)/shard_map/reduce_scatter | solution.py:61
  658.4 26.2 %all_to_all.16 = bf16[32,128,128]{2,1,0:T(8,128)(2,1)S(1)} all-to-all(bf16[32,128,128]{2,1,0:T(8,128)(2,1)S(1)} %stack.8), channel_id=1, replica_groups=mesh['row'=32,'col'=8] {'row'}, dimensions={0} | all-to-all | bytes 2097152 | tf_op jit(solution)/shard_map/all_to_all | solution.py:12
  686.7 5.1 fusion.14
  691.8 5.4 copy.18
  701.9 12.7 %all_gather.11 = bf16[1024,128]{1,0:T(8,128)(2,1)S(1)} all-gather(bf16[128,128]{1,0:T(8,128)(2,1)S(1)} %get-tuple-element.5), channel_id=1, replica_groups=mesh['row'=32,'col'=8] {'col'}, dimensions={0}, use_global_device_ids=true | all-gather | bytes 294912 | tf_op jit(solution)/shard_map/all_gather | solution.py:44
  716.7 4.4 fusion.12
  721.1 5.4 copy.19
  726.5 4.0 fusion
  733.2 234.2 %reduce-scatter.17.cloned.1.call-done = f32[128,128]{1,0:T(8,128)} async-done(((f32[4096,128]{1,0:T(8,128)}), f32[128,128]{1,0:T(8,128)}) %reduce-scatter.17.cloned.1.call-update) | async-done | bytes 65552 | tf_op jit(solution)/shard_map/reduce_scatter | solution.py:61
  (51 shorter events, 44.7 us)
Async XLA Ops:
  6.5 50.4 %copy-start = (bf16[1,1,64,128,128]{4,3,2,1,0:T(8,128)(2,1)S(1)}, bf16[1,1,64,128,128]{4,3,2,1,0:T(8,128)(2,1)}, u32[]{:S(2)}) copy-start(bf16[1,1,64,128,128]{4,3,2,1,0:T(8,128)(2,1)} %param.7) | copy-start | bytes 6291460
  6.5 16.0 %copy-start.3 = (s32[1,1,64]{2,1,0:T(1,128)S(1)}, s32[1,1,64]{2,1,0:T(1,128)}, u32[]{:S(2)}) copy-start(s32[1,1,64]{2,1,0:T(1,128)} %param.9) | copy-start | bytes 772
  8.8 46.0 %all-to-all-start = ((bf16[32,128,128]{2,1,0:T(8,128)(2,1)}), bf16[32,128,128]{2,1,0:T(8,128)(2,1)S(1)}, u32[]{:S(2)}, u32[]{:S(2)}) async-start(bf16[32,128,128]{2,1,0:T(8,128)(2,1)} %stack.6), calls=%async_computation | async-start | bytes 2097152 | tf_op jit(solution)/shard_map/all_to_all | solution.py:12
  21.8 83.3 %reduce-scatter.7.cloned.1.call-start = ((), (), s32[]{:S(2)}) async-start(), calls=%async_computation.9 | async-start | bytes 589824 | tf_op jit(solution)/shard_map/reduce_scatter | solution.py:54
  62.1 5.4 copy-start.2
  72.1 269.5 %reduce-scatter.9.cloned.1.call-start = ((), (), s32[]{:S(2)}) async-start(), calls=%async_computation.10 | async-start | bytes 2162688 | tf_op jit(solution)/shard_map/reduce_scatter | solution.py:61
  103.7 237.9 %copy-start.1 = (f32[128,128]{1,0:T(8,128)S(1)}, f32[128,128]{1,0:T(8,128)}, u32[]{:S(2)}) copy-start(f32[128,128]{1,0:T(8,128)} %param.11) | copy-start | bytes 196612
  103.7 313.7 %reduce-scatter.11.cloned.1.call-start = ((), (), s32[]{:S(2)}) async-start(), calls=%async_computation.11 | async-start | bytes 589824 | tf_op jit(solution)/shard_map/reduce_scatter | solution.py:54
  386.2 271.0 %reduce-scatter.13.cloned.1.call-start = ((), (), s32[]{:S(2)}) async-start(), calls=%async_computation.12 | async-start | bytes 2162688 | tf_op jit(solution)/shard_map/reduce_scatter | solution.py:61
  417.3 315.9 %reduce-scatter.15.cloned.1.call-start = ((), (), s32[]{:S(2)}) async-start(), calls=%async_computation.13 | async-start | bytes 589824 | tf_op jit(solution)/shard_map/reduce_scatter | solution.py:54
  701.8 265.6 %reduce-scatter.17.cloned.1.call-start = ((), (), s32[]{:S(2)}) async-start(), calls=%async_computation.14 | async-start | bytes 2162688 | tf_op jit(solution)/shard_map/reduce_scatter | solution.py:61
Sparse Core Ops, SparseCore 0:
  72.2 27.0 reduce-scatter.6
  103.9 237.6 reduce-scatter.8
  386.3 27.6 reduce-scatter.10
  417.5 239.7 reduce-scatter.12
  701.9 26.6 reduce-scatter.14
  733.3 234.0 reduce-scatter.16
